TPU v7x, 512 devices: a whole 4x8x8 slice. The times are simulated.
512 devices in a mesh: rep: 16 (over x, z_lo, core), dp: 32 (over y, z_hi).
Axes of the slice: x: 4, y: 8, z: 8 (z_hi: 4, z_lo: 2; z = z_hi * 2 + z_lo), core: 2. Of those that a mesh axis runs over, the one named last changes fastest.
Arguments:
- image_features: bfloat16 [65536, 1408], P(('rep', 'dp')), parts along dimension 0, may hold values from -24 to 24
- text_embed: bfloat16 [65536, 512], P(('rep', 'dp')), parts along dimension 0, may hold values from -24 to 24
- image_head: bfloat16 [22528, 512], P(('rep', 'dp')), parts along dimension 0, may hold values from -1 to 3
- logit_scale: float32 [1], replicated, may hold values from 10 to 40
Outputs:
- image_features_grad: bfloat16 [65536, 1408], P(('rep', 'dp')), parts along dimension 0
- text_embed_grad: bfloat16 [65536, 512], P(('rep', 'dp')), parts along dimension 0
- image_head_grad: float32 [22528, 512], P(('rep', 'dp')), parts along dimension 0
There are 16 independent parts, one for each index of `rep`. A program takes and returns all parts, laid end to end along the dimension named above; an argument that names none is the same for every part. Nothing has to cross between parts.
All inputs are finite; a program needn't handle non-finite values.
Results may differ from a plain program's by a relative error of at most 0.02.
Values may be sent and summed in bfloat16 or wider, within the bound.
No kernel may reach another device: no remote copies, remote signals or barrier semaphores. Data moves between devices by JAX's collectives and lax.ppermute only.
A program may use at most 64 MiB of HBM per device.

v0:
```python
import jax
import jax.numpy as jnp
from jax import lax
from jax.sharding import Mesh
from jax.sharding import PartitionSpec as P

DP = ("dp_0", "dp_1")
REP_DP = ("rep", "dp_0", "dp_1")


def from_everyone(array, axis):
    devices = lax.axis_size(axis)
    return lax.all_to_all(
        jnp.broadcast_to(array[None], (devices, *array.shape)), axis, 0, 0, tiled=True
    )


def joined_along(parts, dim):
    shape = list(parts.shape[1:])
    shape[dim] *= parts.shape[0]
    return jnp.moveaxis(parts, 0, dim).reshape(shape)


def collect(array, axis, dim):
    parts = from_everyone(array, axis)
    return joined_along(parts, dim)


def gathered_by_axis(array, axes, dim):
    if not axes:
        return array
    nearer = lax.all_gather(array, axes[-1], axis=dim, tiled=True)
    return gathered_by_axis(nearer, axes[:-1], dim)


def split_up(array, dim, devices):
    before, after = (array.shape[:dim], array.shape[dim + 1 :])
    return jnp.moveaxis(array.reshape(*before, devices, -1, *after), dim, 0)


def sent_and_summed(array, axis, dim):
    devices = lax.axis_size(axis)
    parts = lax.all_to_all(split_up(array, dim, devices), axis, 0, 0, tiled=True)
    return jnp.sum(parts, axis=0)


def rows_first(arrays, axis, dims):
    turned = [jnp.moveaxis(a, dim, 0) for a, dim in zip(arrays, dims)]
    widths = [t[0].size for t in turned]
    both = jnp.concatenate([t.reshape(-1, w) for t, w in zip(turned, widths)], axis=1)
    result = lax.all_gather(both, axis, axis=0, tiled=True)
    parts = jnp.split(result, [sum(widths[:k]) for k in range(1, len(widths))], axis=1)
    return tuple(
        (
            jnp.moveaxis(b.reshape(-1, *t.shape[1:]), 0, dim)
            for b, t, dim in zip(parts, turned, dims)
        )
    )


def summed_on_arrival(array, axis, dim):
    devices = lax.axis_size(axis)
    parts = lax.all_to_all(split_up(array, dim, devices), axis, 0, 0, tiled=True)
    return jnp.sum(parts.astype(jnp.float32), axis=0)


def unit_rows(embedding):
    inv_norm = lax.rsqrt(jnp.sum(embedding * embedding, axis=1, keepdims=True) + 1e-06)
    return (embedding * inv_norm, inv_norm)


def norm_backward(embedding, inv_norm, upstream):
    inner = jnp.sum(embedding * upstream, axis=1, keepdims=True)
    return (inv_norm * upstream - embedding * (inv_norm * inv_norm * inv_norm) * inner).astype(
        jnp.bfloat16
    )


def tile_logits(logit_mult, left_rows, right_rows):
    product = lax.dot_general(
        left_rows, right_rows, (((1,), (1,)), ((), ())), preferred_element_type=jnp.float32
    )
    return logit_mult * product


def pair_coef(logits, left_lse, right_lse, left_ids, right_ids):
    label = (left_ids[:, None] == right_ids[None, :]).astype(jnp.float32)
    values = (
        jnp.exp(logits - left_lse[:, None]) + jnp.exp(logits - right_lse[None, :]) - 2.0 * label
    )
    return values.astype(jnp.bfloat16)


def local(image_features, text_embed, image_head, logit_scale):
    logit_mult = logit_scale[0]
    row_count = image_features.shape[0]
    batch_total = row_count * lax.axis_size(DP)
    own_ids = lax.axis_index(DP) * row_count + jnp.arange(row_count, dtype=jnp.int32)
    head_full = collect(image_head, DP, 0)
    img_emb = jnp.dot(image_features, head_full, preferred_element_type=jnp.float32)
    img_scaled, img_inv = unit_rows(img_emb)
    img_unit = img_scaled.astype(jnp.bfloat16)
    txt_emb = text_embed.astype(jnp.float32)
    txt_scaled, txt_inv = unit_rows(txt_emb)
    txt_unit = txt_scaled.astype(jnp.bfloat16)
    text_all = gathered_by_axis(txt_unit, DP, 0)
    exp_tile = jnp.exp(tile_logits(logit_mult, img_unit, text_all))
    col_part = jnp.sum(exp_tile, axis=0)
    row_sum, col_part = (jnp.sum(exp_tile, axis=1), col_part)
    row_lse = jnp.log(row_sum)
    col_lse = jnp.log(sent_and_summed(col_part, DP, 0))
    row_all, col_all = rows_first((row_lse, col_lse), DP, (0, 0))
    all_ids = jnp.arange(batch_total, dtype=jnp.int32)
    img_coef = pair_coef(
        tile_logits(logit_mult, img_unit, text_all), row_lse, col_all, own_ids, all_ids
    )
    img_sum = jnp.dot(img_coef, text_all, preferred_element_type=jnp.float32)
    units = lax.all_gather(img_unit, DP, axis=0, tiled=True)
    piece_ids = jnp.arange(units.shape[0], dtype=jnp.int32)
    txt_coef = pair_coef(
        tile_logits(logit_mult, txt_unit, units), col_lse, row_all, own_ids, piece_ids
    )
    txt_sum = jnp.dot(txt_coef, units, preferred_element_type=jnp.float32)
    img_unit_grad = logit_mult * img_sum
    txt_unit_grad = logit_mult * txt_sum
    img_emb_grad = norm_backward(img_emb, img_inv, img_unit_grad)
    text_embed_grad = norm_backward(txt_emb, txt_inv, txt_unit_grad)
    image_features_grad = lax.dot_general(
        img_emb_grad, head_full, (((1,), (1,)), ((), ())), preferred_element_type=jnp.float32
    ).astype(jnp.bfloat16)
    head_partial = lax.dot_general(
        image_features, img_emb_grad, (((0,), (0,)), ((), ())), preferred_element_type=jnp.float32
    )
    image_head_grad = summed_on_arrival(head_partial.astype(jnp.bfloat16), DP, 0)
    return (image_features_grad, text_embed_grad, image_head_grad)


def solution(mesh):
    split = Mesh(mesh.devices.reshape(mesh.shape["rep"], 8, 4), ("rep", "dp_0", "dp_1"))
    return jax.shard_map(
        local,
        mesh=split,
        in_specs=(P(REP_DP, None), P(REP_DP, None), P(REP_DP, None), P()),
        out_specs=(P(REP_DP, None), P(REP_DP, None), P(REP_DP, None)),
        check_vma=False,
    )
```

profile of v0, /device:TPU:6, one launch (start us, length us, event | category | flops | bytes accessed | tf_op | source)
XLA Modules:
  0.0 281.0 jit_solution(6966936409692230886)
XLA Ops:
  7.2 1.1 fusion.9
  8.3 1.0 fusion.10
  9.3 22.3 %all_gather.12 = bf16[512,512]{1,0:T(8,128)(2,1)} all-gather(bf16[128,512]{1,0:T(8,128)(2,1)S(1)} %fusion.10), channel_id=1, replica_groups=mesh['rep'=16,'dp_0'=8,'dp_1'=4] {'dp_1'}, dimensions={0}, use_global_device_ids=true | all-gather | bytes 655360 | tf_op jit(solution)/shard_map/all_gather | solution.py:32
  31.7 1.0 broadcast_in_dim.2
  32.6 64.9 %all_to_all.19 = bf16[32,44,512]{2,1,0:T(8,128)(2,1)S(1)} all-to-all(bf16[32,44,512]{2,1,0:T(8,128)(2,1)S(1)} %broadcast_in_dim.2), channel_id=1, replica_groups=mesh['rep'=16,'dp_0'=8,'dp_1'=4] {'dp_0','dp_1'}, dimensions={0} | all-to-all | bytes 2883584 | tf_op jit(solution)/shard_map/all_to_all | solution.py:13
  97.6 0.3 reshape.67
  97.9 0.5 multiply_reduce_fusion.1
  98.4 0.8 multiply_convert_fusion
  99.8 17.5 %all-gather.3.cloned.1.call-done = bf16[4096,512]{1,0:T(8,128)(2,1)} async-done(((bf16[512,512]{1,0:T(8,128)(2,1)}), bf16[4096,512]{1,0:T(8,128)(2,1)}) %all-gather.3.cloned.1.call-update) | async-done | bytes 4194320 | tf_op jit(solution)/shard_map/all_gather | solution.py:32
  117.3 5.7 %exponential_reduce_fusion.1 = (f32[128]{0:T(128)S(1)}, f32[4096]{0:T(1024)}, f32[128,4096]{1,0:T(8,128)}) fusion(bf16[128,512]{1,0:T(8,128)(2,1)} %multiply_convert_fusion, bf16[4096,512]{1,0:T(8,128)(2,1)} %all-gather.3.cloned.1.call-done, f32[]{:T(128)} %bitcast.24), kind=kOutput, calls=%fused_computation.12 | convolution fusion | flops 538439552 | bytes 6439428 | tf_op jit(solution)/shard_map/dot_general | solution.py:80
  123.0 9.7 %all-to-all-start.1 = ((f32[32,1,128]{2,1,0:T(1,128)}), f32[32,1,128]{2,1,0:T(1,128)S(1)}, u32[]{:S(2)}, u32[]{:S(2)}) async-start(f32[32,1,128]{2,1,0:T(1,128)} %bitcast.2), calls=%async_computation.1 | async-start | bytes 32768 | tf_op jit(solution)/shard_map/all_to_all | solution.py:43
  132.7 12.1 %all-to-all-done.1 = f32[32,1,128]{2,1,0:T(1,128)S(1)} async-done(((f32[32,1,128]{2,1,0:T(1,128)}), f32[32,1,128]{2,1,0:T(1,128)S(1)}, u32[]{:S(2)}, u32[]{:S(2)}) %all-to-all-start.1) | async-done | bytes 16416 | tf_op jit(solution)/shard_map/all_to_all | solution.py:43
  144.9 76.4 %all_gather.14 = f32[4096,2]{0,1:T(2,128)S(1)} all-gather(f32[128,2]{0,1:T(2,128)S(1)} %pad_maximum_fusion), channel_id=1, replica_groups=mesh['rep'=16,'dp_0'=8,'dp_1'=4] {'dp_0','dp_1'}, dimensions={0}, use_global_device_ids=true | all-gather | bytes 33792 | tf_op jit(solution)/shard_map/all_gather | solution.py:51
  221.3 3.9 %multiply_reduce_fusion = (f32[128]{0:T(128)S(1)}, f32[128,512]{1,0:T(8,128)S(1)}) fusion(f32[128,512]{1,0:T(8,128)S(1)} %get-tuple-element.16, bf16[4096,512]{1,0:T(8,128)(2,1)} %all-gather.3.cloned.1.call-done, f32[128,4096]{1,0:T(8,128)} %get-tuple-element.17, s32[128]{0:T(128)S(1)} %iota_add_fusion, f32[4096]{0:T(1024)S(1)} %bitcast.28, ...), kind=kOutput, calls=%fused_computation.31 | convolution fusion | flops 540737408 | bytes 6833668 | tf_op jit(solution)/shard_map/dot_general | solution.py:117
  225.3 0.6 copy-done.2
  226.0 1.7 fusion
  227.6 1.7 copy.10
  229.3 1.3 reshape.68
  230.6 5.2 %all-to-all-start.2 = ((bf16[32,44,512]{2,1,0:T(8,128)(2,1)}), bf16[32,44,512]{2,1,0:T(8,128)(2,1)S(1)}, u32[]{:S(2)}, u32[]{:S(2)}) async-start(bf16[32,44,512]{2,1,0:T(8,128)(2,1)} %reshape.68), calls=%async_computation.2 | async-start | bytes 3145728 | tf_op jit(solution)/shard_map/all_to_all | solution.py:63
  235.9 2.3 convolution_convert_fusion.1
  238.2 28.6 %all-to-all-done.2 = bf16[32,44,512]{2,1,0:T(8,128)(2,1)S(1)} async-done(((bf16[32,44,512]{2,1,0:T(8,128)(2,1)}), bf16[32,44,512]{2,1,0:T(8,128)(2,1)S(1)}, u32[]{:S(2)}, u32[]{:S(2)}) %all-to-all-start.2) | async-done | bytes 1441824 | tf_op jit(solution)/shard_map/all_to_all | solution.py:63
  266.8 0.9 convert_reduce_fusion
  267.7 5.7 %fusion.14 = (f32[128]{0:T(128)S(1)}, f32[128,512]{1,0:T(8,128)S(1)}) fusion(bf16[128,512]{1,0:T(8,128)(2,1)S(1)} %copy-done.1, bf16[4096,512]{1,0:T(8,128)(2,1)} %all-gather.5.cloned.1.call-done, bf16[128,512]{1,0:T(8,128)(2,1)} %copy-done.3, f32[4096]{0:T(1024)S(1)} %bitcast.27, f32[128]{0:T(128)S(1)} %get-tuple-element.9, s32[128]{0:T(128)S(1)} %iota_add_fusion, ...), kind=kOutput, calls=%fused_computation.29 | convolution fusion | flops 1078198144 | bytes 4736516 | tf_op jit(solution)/shard_map/dot_general | solution.py:123
  273.3 0.8 fusion.13
  (21 shorter events, 0.4 us)
Async XLA Ops:
  7.2 90.7 %copy-start = (bf16[128,1408]{1,0:T(8,128)(2,1)S(1)}, bf16[128,1408]{1,0:T(8,128)(2,1)}, u32[]{:S(2)}) copy-start(bf16[128,1408]{1,0:T(8,128)(2,1)} %param.4) | copy-start | bytes 1081348
  7.2 110.1 %all-gather.3.cloned.1.call-start = ((), (), s32[]{:S(2)}) async-start(), calls=%async_computation.3 | async-start | bytes 4718592 | tf_op jit(solution)/shard_map/all_gather | solution.py:32
  9.3 23.3 %copy-start.3 = (bf16[128,512]{1,0:T(8,128)(2,1)}, bf16[128,512]{1,0:T(8,128)(2,1)S(1)}, u32[]{:S(2)}) copy-start(bf16[128,512]{1,0:T(8,128)(2,1)S(1)} %fusion.10) | copy-start | bytes 393220
  31.6 236.1 %all-gather.5.cloned.1.call-start = ((), (), s32[]{:S(2)}) async-start(), calls=%async_computation.4 | async-start | bytes 4325376 | tf_op jit(solution)/shard_map/all_gather | solution.py:118
  123.0 21.8 %all-to-all-start.1 = ((f32[32,1,128]{2,1,0:T(1,128)}), f32[32,1,128]{2,1,0:T(1,128)S(1)}, u32[]{:S(2)}, u32[]{:S(2)}) async-start(f32[32,1,128]{2,1,0:T(1,128)} %bitcast.2), calls=%async_computation.1 | async-start | bytes 32768 | tf_op jit(solution)/shard_map/all_to_all | solution.py:43
  225.3 0.7 copy-start.2
  230.6 36.1 %all-to-all-start.2 = ((bf16[32,44,512]{2,1,0:T(8,128)(2,1)}), bf16[32,44,512]{2,1,0:T(8,128)(2,1)S(1)}, u32[]{:S(2)}, u32[]{:S(2)}) async-start(bf16[32,44,512]{2,1,0:T(8,128)(2,1)} %reshape.68), calls=%async_computation.2 | async-start | bytes 3145728 | tf_op jit(solution)/shard_map/all_to_all | solution.py:63
  235.9 31.8 %copy-start.1 = (bf16[128,512]{1,0:T(8,128)(2,1)S(1)}, bf16[128,512]{1,0:T(8,128)(2,1)}, u32[]{:S(2)}) copy-start(bf16[128,512]{1,0:T(8,128)(2,1)} %param.5) | copy-start | bytes 393220
Sparse Core Ops, SparseCore 0:
  31.7 85.5 all-gather.2
  121.0 101.9 all-gather.4
where the time goes:
time: 281 us
  blocking collectives  164 us (58%)
  waiting for transfers between devices  58.2 us (21%)
  matrix products  19.7 us (7%)
  starting transfers between devices  15 us (5%)
  between operations  14.8 us (5%)
  local copies, waits for them, and re-layouts  4.97 us (2%)
  other arithmetic  4.66 us (2%)
    all_gather x1, blocking collectives, rows_first(): result = lax.all_gather(both, axis, axis=0, tiled=True)  76.4 us
    all_to_all x1, blocking collectives, from_everyone(): lax.all_to_all(jnp.broadcast_to(array[None], (devices, *array.shape)), ax...  64.9 us
    all_to_all x1, waiting for transfers between devices, summed_on_arrival(): lax.all_to_all(split_up(array, dim, devices), axis, 0, 0, tiled=True)  28.6 us
    all_gather x1, blocking collectives, gathered_by_axis(): nearer = lax.all_gather(array, axes[-1], axis=dim, tiled=True)  22.3 us
    all_gather x1, waiting for transfers between devices, gathered_by_axis(): nearer = lax.all_gather(array, axes[-1], axis=dim, tiled=True)  17.5 us
    all_to_all x1, waiting for transfers between devices, sent_and_summed(): lax.all_to_all(split_up(array, dim, devices), axis, 0, 0, tiled=True)  12.1 us
    all_to_all x1, starting transfers between devices, sent_and_summed(): lax.all_to_all(split_up(array, dim, devices), axis, 0, 0, tiled=True)  9.68 us
    dot_general x1, matrix products, tile_logits(): lax.dot_general(left_rows, right_rows, (((1,), (1,)), ((), ())), preferre...  5.75 us
  transfers between devices with their start and end apart: 4, of which 3 were waited for; matrix products, arithmetic and copies ran while one was open for 7% of the time, Pallas kernels for 0%

commit v1 on v0

--- a/solution.py
+++ b/solution.py
@@ -48,7 +48,9 @@
     turned = [jnp.moveaxis(a, dim, 0) for a, dim in zip(arrays, dims)]
     widths = [t[0].size for t in turned]
     both = jnp.concatenate([t.reshape(-1, w) for t, w in zip(turned, widths)], axis=1)
-    result = lax.all_gather(both, axis, axis=0, tiled=True)
+    result = jnp.concatenate(
+        lax.all_to_all(jnp.stack([both] * lax.axis_size(axis)), axis, 0, 0), axis=0
+    )
     parts = jnp.split(result, [sum(widths[:k]) for k in range(1, len(widths))], axis=1)
     return tuple(
         (

time: 281 us -> 270 us (0.961)
  blocking collectives: 164 us -> 87.2 us
  waiting for transfers between devices: 58.2 us -> 120 us
    all_gather x1 -> x0, blocking collectives: 76.4 us -> none  [rows_first(): result = lax.all_gather(both, axis, axis=0, tiled=True)]
    all_gather x1, waiting for transfers between devices: 0.01 us -> 35 us  [local(): units = lax.all_gather(img_unit, DP, axis=0, tiled=True)]
    all_to_all x1, waiting for transfers between devices: 28.6 us -> 42.8 us  [summed_on_arrival(): lax.all_to_all(split_up(array, dim, devices), axis, 0, 0, tiled=True)]
    all_to_all x0 -> x1, waiting for transfers between devices: none -> 12.2 us  [rows_first(): lax.all_to_all(jnp.stack([both] * lax.axis_size(axis)), axis, 0, 0)]
    all_to_all x0 -> x1, starting transfers between devices: none -> 3.85 us  [rows_first(): lax.all_to_all(jnp.stack([both] * lax.axis_size(axis)), axis, 0, 0)]
  transfers between devices with their start and end apart: 4 -> 5, of which waited for: 3 -> 5; matrix products, arithmetic and copies ran while one was open for 7% -> 8% of each run, Pallas kernels for 0% -> 0%
where the time goes in v1:
time: 270 us; the launch traced here: 269 us
  waiting for transfers between devices  120 us (44%)
  blocking collectives  87.2 us (32%)
  matrix products  19.7 us (7%)
  starting transfers between devices  17.6 us (7%)
  between operations  14.8 us (5%)
  local copies, waits for them, and re-layouts  5.61 us (2%)
  other arithmetic  4.66 us (2%)
    all_to_all x1, blocking collectives, from_everyone(): lax.all_to_all(jnp.broadcast_to(array[None], (devices, *array.shape)), ax...  64.9 us
    all_to_all x1, waiting for transfers between devices, summed_on_arrival(): lax.all_to_all(split_up(array, dim, devices), axis, 0, 0, tiled=True)  42.8 us
    all_gather x1, waiting for transfers between devices, local(): units = lax.all_gather(img_unit, DP, axis=0, tiled=True)  35 us
    all_gather x1, blocking collectives, gathered_by_axis(): nearer = lax.all_gather(array, axes[-1], axis=dim, tiled=True)  22.3 us
    all_gather x1, waiting for transfers between devices, gathered_by_axis(): nearer = lax.all_gather(array, axes[-1], axis=dim, tiled=True)  17.5 us
    all_to_all x1, waiting for transfers between devices, rows_first(): lax.all_to_all(jnp.stack([both] * lax.axis_size(axis)), axis, 0, 0)  12.2 us
    all_to_all x1, waiting for transfers between devices, sent_and_summed(): lax.all_to_all(split_up(array, dim, devices), axis, 0, 0, tiled=True)  12.1 us
    all_to_all x1, starting transfers between devices, sent_and_summed(): lax.all_to_all(split_up(array, dim, devices), axis, 0, 0, tiled=True)  9.68 us
  transfers between devices with their start and end apart: 5, of which 5 were waited for; matrix products, arithmetic and copies ran while one was open for 8% of the time, Pallas kernels for 0%

profile of v1, /device:TPU:6, one launch (start us, length us, event | category | flops | bytes accessed | tf_op | source)
XLA Modules:
  0.0 269.2 jit_solution(5607981453867302120)
XLA Ops:
  7.2 1.1 fusion.9
  8.3 1.0 fusion.10
  9.3 22.3 %all_gather.9 = bf16[512,512]{1,0:T(8,128)(2,1)} all-gather(bf16[128,512]{1,0:T(8,128)(2,1)S(1)} %fusion.10), channel_id=1, replica_groups=mesh['rep'=16,'dp_0'=8,'dp_1'=4] {'dp_1'}, dimensions={0}, use_global_device_ids=true | all-gather | bytes 655360 | tf_op jit(solution)/shard_map/all_gather | solution.py:32
  31.7 1.0 broadcast_in_dim.2
  32.6 64.9 %all_to_all.24 = bf16[32,44,512]{2,1,0:T(8,128)(2,1)S(1)} all-to-all(bf16[32,44,512]{2,1,0:T(8,128)(2,1)S(1)} %broadcast_in_dim.2), channel_id=1, replica_groups=mesh['rep'=16,'dp_0'=8,'dp_1'=4] {'dp_0','dp_1'}, dimensions={0} | all-to-all | bytes 2883584 | tf_op jit(solution)/shard_map/all_to_all | solution.py:13
  98.4 0.8 multiply_convert_fusion
  99.8 17.5 %all-gather.3.cloned.1.call-done = bf16[4096,512]{1,0:T(8,128)(2,1)} async-done(((bf16[512,512]{1,0:T(8,128)(2,1)}), bf16[4096,512]{1,0:T(8,128)(2,1)}) %all-gather.3.cloned.1.call-update) | async-done | bytes 4194320 | tf_op jit(solution)/shard_map/all_gather | solution.py:32
  117.3 5.7 %exponential_reduce_fusion.1 = (f32[128]{0:T(128)S(1)}, f32[4096]{0:T(1024)}, f32[128,4096]{1,0:T(8,128)}) fusion(bf16[128,512]{1,0:T(8,128)(2,1)} %multiply_convert_fusion, bf16[4096,512]{1,0:T(8,128)(2,1)} %all-gather.3.cloned.1.call-done, f32[]{:T(128)} %bitcast.25), kind=kOutput, calls=%fused_computation.12 | convolution fusion | flops 538439552 | bytes 6439428 | tf_op jit(solution)/shard_map/dot_general | solution.py:82
  123.0 9.7 %all-to-all-start.1 = ((f32[32,1,128]{2,1,0:T(1,128)}), f32[32,1,128]{2,1,0:T(1,128)S(1)}, u32[]{:S(2)}, u32[]{:S(2)}) async-start(f32[32,1,128]{2,1,0:T(1,128)} %bitcast.2), calls=%async_computation.1 | async-start | bytes 32768 | tf_op jit(solution)/shard_map/all_to_all | solution.py:43
  132.7 12.1 %all-to-all-done.1 = f32[32,1,128]{2,1,0:T(1,128)S(1)} async-done(((f32[32,1,128]{2,1,0:T(1,128)}), f32[32,1,128]{2,1,0:T(1,128)S(1)}, u32[]{:S(2)}, u32[]{:S(2)}) %all-to-all-start.1) | async-done | bytes 16416 | tf_op jit(solution)/shard_map/all_to_all | solution.py:43
  145.5 3.9 %all-to-all-start.2 = ((f32[32,128,2]{1,2,0:T(2,128)}), f32[32,128,2]{1,2,0:T(2,128)S(1)}, u32[]{:S(2)}, u32[]{:S(2)}) async-start(f32[32,128,2]{1,2,0:T(2,128)} %stack.2), calls=%async_computation.2 | async-start | bytes 65536 | tf_op jit(solution)/shard_map/all_to_all | solution.py:52
  149.3 12.2 %all-to-all-done.2 = f32[32,128,2]{1,2,0:T(2,128)S(1)} async-done(((f32[32,128,2]{1,2,0:T(2,128)}), f32[32,128,2]{1,2,0:T(2,128)S(1)}, u32[]{:S(2)}, u32[]{:S(2)}) %all-to-all-start.2) | async-done | bytes 32800 | tf_op jit(solution)/shard_map/all_to_all | solution.py:52
  161.6 3.9 %multiply_reduce_fusion = (f32[128]{0:T(128)S(1)}, f32[128,512]{1,0:T(8,128)S(1)}) fusion(f32[128,512]{1,0:T(8,128)S(1)} %get-tuple-element.16, bf16[4096,512]{1,0:T(8,128)(2,1)} %all-gather.3.cloned.1.call-done, f32[128,4096]{1,0:T(8,128)} %get-tuple-element.17, s32[128]{0:T(128)S(1)} %iota_add_fusion, f32[4096]{0:T(1024)S(1)} %bitcast.30, ...), kind=kOutput, calls=%fused_computation.31 | convolution fusion | flops 540737408 | bytes 6833668 | tf_op jit(solution)/shard_map/dot_general | solution.py:119
  165.6 0.6 copy-done.2
  166.2 1.7 fusion
  167.9 1.7 copy.12
  169.6 1.3 reshape.74
  170.9 4.0 %all-to-all-start.3 = ((bf16[32,44,512]{2,1,0:T(8,128)(2,1)}), bf16[32,44,512]{2,1,0:T(8,128)(2,1)S(1)}, u32[]{:S(2)}, u32[]{:S(2)}) async-start(bf16[32,44,512]{2,1,0:T(8,128)(2,1)} %reshape.74), calls=%async_computation.3 | async-start | bytes 3145728 | tf_op jit(solution)/shard_map/all_to_all | solution.py:65
  174.9 2.3 convolution_convert_fusion.1
  177.2 42.8 %all-to-all-done.3 = bf16[32,44,512]{2,1,0:T(8,128)(2,1)S(1)} async-done(((bf16[32,44,512]{2,1,0:T(8,128)(2,1)}), bf16[32,44,512]{2,1,0:T(8,128)(2,1)S(1)}, u32[]{:S(2)}, u32[]{:S(2)}) %all-to-all-start.3) | async-done | bytes 1441824 | tf_op jit(solution)/shard_map/all_to_all | solution.py:65
  220.0 0.9 convert_reduce_fusion
  220.9 35.0 %all-gather.5.cloned.1.call-done = bf16[4096,512]{1,0:T(8,128)(2,1)} async-done(((bf16[128,512]{1,0:T(8,128)(2,1)}), bf16[4096,512]{1,0:T(8,128)(2,1)}) %all-gather.5.cloned.1.call-update) | async-done | bytes 4194320 | tf_op jit(solution)/shard_map/all_gather | solution.py:120
  255.9 5.7 %fusion.14 = (f32[128]{0:T(128)S(1)}, f32[128,512]{1,0:T(8,128)S(1)}) fusion(bf16[128,512]{1,0:T(8,128)(2,1)S(1)} %copy-done.1, bf16[4096,512]{1,0:T(8,128)(2,1)} %all-gather.5.cloned.1.call-done, bf16[128,512]{1,0:T(8,128)(2,1)} %copy-done.3, f32[4096]{0:T(1024)S(1)} %bitcast.29, f32[128]{0:T(128)S(1)} %get-tuple-element.9, s32[128]{0:T(128)S(1)} %iota_add_fusion, ...), kind=kOutput, calls=%fused_computation.29 | convolution fusion | flops 1078198144 | bytes 4736516 | tf_op jit(solution)/shard_map/dot_general | solution.py:125
  261.6 0.8 fusion.13
  (23 shorter events, 1.7 us)
Async XLA Ops:
  7.2 90.7 %copy-start = (bf16[128,1408]{1,0:T(8,128)(2,1)S(1)}, bf16[128,1408]{1,0:T(8,128)(2,1)}, u32[]{:S(2)}) copy-start(bf16[128,1408]{1,0:T(8,128)(2,1)} %param.4) | copy-start | bytes 1081348
  7.2 110.1 %all-gather.3.cloned.1.call-start = ((), (), s32[]{:S(2)}) async-start(), calls=%async_computation.4 | async-start | bytes 4718592 | tf_op jit(solution)/shard_map/all_gather | solution.py:32
  9.3 23.3 %copy-start.3 = (bf16[128,512]{1,0:T(8,128)(2,1)}, bf16[128,512]{1,0:T(8,128)(2,1)S(1)}, u32[]{:S(2)}) copy-start(bf16[128,512]{1,0:T(8,128)(2,1)S(1)} %fusion.10) | copy-start | bytes 393220
  31.6 224.3 %all-gather.5.cloned.1.call-start = ((), (), s32[]{:S(2)}) async-start(), calls=%async_computation.5 | async-start | bytes 4325376 | tf_op jit(solution)/shard_map/all_gather | solution.py:120
  123.0 21.8 %all-to-all-start.1 = ((f32[32,1,128]{2,1,0:T(1,128)}), f32[32,1,128]{2,1,0:T(1,128)S(1)}, u32[]{:S(2)}, u32[]{:S(2)}) async-start(f32[32,1,128]{2,1,0:T(1,128)} %bitcast.2), calls=%async_computation.1 | async-start | bytes 32768 | tf_op jit(solution)/shard_map/all_to_all | solution.py:43
  145.5 16.1 %all-to-all-start.2 = ((f32[32,128,2]{1,2,0:T(2,128)}), f32[32,128,2]{1,2,0:T(2,128)S(1)}, u32[]{:S(2)}, u32[]{:S(2)}) async-start(f32[32,128,2]{1,2,0:T(2,128)} %stack.2), calls=%async_computation.2 | async-start | bytes 65536 | tf_op jit(solution)/shard_map/all_to_all | solution.py:52
  165.6 0.7 copy-start.2
  170.9 49.1 %all-to-all-start.3 = ((bf16[32,44,512]{2,1,0:T(8,128)(2,1)}), bf16[32,44,512]{2,1,0:T(8,128)(2,1)S(1)}, u32[]{:S(2)}, u32[]{:S(2)}) async-start(bf16[32,44,512]{2,1,0:T(8,128)(2,1)} %reshape.74), calls=%async_computation.3 | async-start | bytes 3145728 | tf_op jit(solution)/shard_map/all_to_all | solution.py:65
  174.9 81.0 %copy-start.1 = (bf16[128,512]{1,0:T(8,128)(2,1)S(1)}, bf16[128,512]{1,0:T(8,128)(2,1)}, u32[]{:S(2)}) copy-start(bf16[128,512]{1,0:T(8,128)(2,1)} %param.5) | copy-start | bytes 393220
Sparse Core Ops, SparseCore 0:
  31.7 85.5 all-gather.2
  121.0 134.8 all-gather.4
